TPU v7x, 32 devices: a whole 2x2x4 slice. The times are simulated.
32 devices in a mesh: freq: 2 (over y), harm: 4 (over z), wall: 4 (over x, core).
Axes of the slice: x: 2, y: 2, z: 4, core: 2. Of those that a mesh axis runs over, the one named last changes fastest.
Arguments:
- sketch: bfloat16 [32, 1024, 128], P(('freq', 'harm'), 'wall'), parts along dimension 0, may hold values from -48 to 48
- inverse_blocks: bfloat16 [32, 1024, 1024], P(('freq', 'harm'), 'wall'), parts along dimension 0, may hold values from -0.1875 to 0.1875
- couple_up: bfloat16 [8, 1024, 1024], P('freq', 'wall'), parts along dimension 0, may hold values from -0.03125 to 0.03125
- couple_down: bfloat16 [8, 1024, 1024], P('freq', 'wall'), parts along dimension 0, may hold values from -0.03125 to 0.03125
- strip_harmonics: int32 [8], P('freq'), parts along dimension 0, may hold values from 0 to 3
Outputs:
- basis: float32 [32, 1024, 128], P(('freq', 'harm'), 'wall'), parts along dimension 0
- triangle: float32 [256, 128], P('freq'), parts along dimension 0
There are 2 independent parts, one for each index of `freq`. A program takes and returns all parts, laid end to end along the dimension named above; each array names one. Nothing has to cross between parts.
Inputs may be any that keep to these rules, and one draw needn't show every extreme that they name: `strip_harmonics`: each entry one of 0 to 3; entries may repeat.
All inputs are finite; a program needn't handle non-finite values.
Results may differ from a plain program's by a relative error of at most 0.0045.
Values may be sent and summed in bfloat16 or wider, within the bound.
A program may use at most 64 MiB of HBM per device.

v0:
```python
import jax
import jax.numpy as jnp
from jax import lax
from jax.sharding import PartitionSpec as P

BAND = 4
SWEEPS = 3


def padded(cells, sides, width):
    for axis, dim in sides:
        count = lax.axis_size(axis)
        head = lax.slice_in_dim(cells, 0, width, axis=dim)
        tail = lax.slice_in_dim(cells, cells.shape[dim] - width, cells.shape[dim], axis=dim)
        cells = jnp.concatenate(
            [
                lax.ppermute(tail, axis, [(i, (i + 1) % count) for i in range(count)]),
                cells,
                lax.ppermute(head, axis, [((i + 1) % count, i) for i in range(count)]),
            ],
            axis=dim,
        )
    return cells


def body(sketch, inverse_blocks, couple_up, couple_down, strip_harmonics):
    offsets = strip_harmonics + 1
    local_count = sketch.shape[0]
    row_count = sketch.shape[1]
    width = sketch.shape[2]
    empty = jnp.zeros((local_count, row_count, width), jnp.float32)

    def add_inverse(piece):
        return jnp.einsum("hrc,hck->hrk", inverse_blocks, piece, preferred_element_type=jnp.float32)

    def apply_inverse(source):
        return add_inverse(lax.all_gather(source, "wall", axis=1, tiled=True))

    state = apply_inverse(sketch).astype(jnp.bfloat16)
    sampled = None
    for sweep in range(SWEEPS):
        extended = padded(state, (("harm", 0),), BAND)
        total = empty
        add_piece = lax.all_gather(extended, "wall", axis=1, tiled=True)
        for j in range(BAND):
            up_cols = couple_up[j]
            down_cols = couple_down[j]
            below = lax.dynamic_slice_in_dim(add_piece, BAND - offsets[j], local_count, 0)
            above = lax.dynamic_slice_in_dim(add_piece, BAND + offsets[j], local_count, 0)
            total = total + jnp.einsum(
                "rc,hck->hrk", up_cols, below, preferred_element_type=jnp.float32
            )
            total = total + jnp.einsum(
                "rc,hck->hrk", down_cols, above, preferred_element_type=jnp.float32
            )
        rhs = (sketch.astype(jnp.float32) - total).astype(jnp.bfloat16)
        result = apply_inverse(rhs)
        if sweep < SWEEPS - 1:
            state = result.astype(jnp.bfloat16)
        else:
            sampled = result
    flat = sampled.reshape(local_count * row_count, width)
    count = lax.axis_size("harm") * lax.axis_size("wall") * local_count * row_count
    local_gram = jnp.dot(
        flat.T, flat, precision=lax.Precision.HIGHEST, preferred_element_type=jnp.float32
    )
    gram = lax.psum(local_gram, ("harm", "wall")) / count
    lower = jnp.linalg.cholesky(gram)
    basis = jax.scipy.linalg.solve_triangular(lower, flat.T, lower=True).T
    triangle = lower.T
    return (basis.reshape(local_count, row_count, width), triangle)


def solution(mesh):
    return jax.shard_map(
        body,
        mesh=mesh,
        in_specs=(
            P(("freq", "harm"), "wall", None),
            P(("freq", "harm"), "wall", None),
            P("freq", "wall", None),
            P("freq", "wall", None),
            P("freq"),
        ),
        out_specs=(P(("freq", "harm"), "wall", None), P("freq", None)),
        check_vma=False,
    )
```

profile of v0, /device:TPU:8, one launch (start us, length us, event | category | flops | bytes accessed | tf_op | source)
XLA Modules:
  0.0 370.6 jit_solution(4480394632407928866)
XLA Ops:
  7.2 0.7 all-gather.8.cloned.1.call-update
  8.0 19.5 %all-gather.8.cloned.1.call-done = bf16[4,1024,128]{2,1,0:T(8,128)(2,1)} async-done(((bf16[4,256,128]{2,1,0:T(8,128)(2,1)}), bf16[4,1024,128]{2,1,0:T(8,128)(2,1)}) %all-gather.8.cloned.1.call-update) | async-done | bytes 1048592 | tf_op jit(solution)/shard_map/all_gather | solution.py:37
  27.4 1.9 convolution_convert_fusion.2
  29.4 0.6 collective-permute-start.1
  30.0 1.5 collective-permute-start
  31.5 6.4 %collective-permute-done.1 = bf16[4,256,128]{2,1,0:T(8,128)(2,1)S(1)} collective-permute-done((bf16[4,256,128]{2,1,0:T(8,128)(2,1)S(1)}, bf16[4,256,128]{2,1,0:T(8,128)(2,1)S(1)}, u32[]{:S(2)}, u32[]{:S(2)}) %collective-permute-start.1) | collective-permute-done | bytes 262176 | tf_op jit(solution)/shard_map/ppermute | solution.py:19
  37.9 7.5 %collective-permute-done = bf16[4,256,128]{2,1,0:T(8,128)(2,1)S(1)} collective-permute-done((bf16[4,256,128]{2,1,0:T(8,128)(2,1)S(1)}, bf16[4,256,128]{2,1,0:T(8,128)(2,1)S(1)}, u32[]{:S(2)}, u32[]{:S(2)}) %collective-permute-start) | collective-permute-done | bytes 262176 | tf_op jit(solution)/shard_map/ppermute | solution.py:17
  45.4 1.0 pad_maximum_fusion
  46.4 0.7 fusion.114
  57.1 0.1 copy.7
  57.3 16.1 %all-gather.10.cloned.1.call-done = bf16[12,1024,128]{2,1,0:T(8,128)(2,1)} async-done(((bf16[12,256,128]{2,1,0:T(8,128)(2,1)}), bf16[12,1024,128]{2,1,0:T(8,128)(2,1)}) %all-gather.10.cloned.1.call-update) | async-done | bytes 3145744 | tf_op jit(solution)/shard_map/all_gather | solution.py:44
  73.4 2.0 fusion.35
  75.5 1.9 convolution_add_fusion.20
  77.3 1.7 convolution_add_fusion.19
  79.1 0.5 convolution_add_fusion.18
  79.6 0.5 convolution_add_fusion.17
  80.1 0.5 convolution_add_fusion.16
  80.6 0.5 convolution_add_fusion.15
  81.1 1.2 fusion.8
  82.3 16.9 %all-gather.12.cloned.1.call-done = bf16[4,1024,128]{1,2,0:T(8,128)(2,1)} async-done(((bf16[4,256,128]{1,2,0:T(8,128)(2,1)}), bf16[4,1024,128]{1,2,0:T(8,128)(2,1)}) %all-gather.12.cloned.1.call-update) | async-done | bytes 1048592 | tf_op jit(solution)/shard_map/all_gather | solution.py:37
  99.3 2.1 fusion.9
  101.3 0.6 collective-permute-start.3
  101.9 1.5 collective-permute-start.2
  103.4 6.4 %collective-permute-done.3 = bf16[4,256,128]{1,2,0:T(8,128)(2,1)S(1)} collective-permute-done((bf16[4,256,128]{1,2,0:T(8,128)(2,1)S(1)}, bf16[4,256,128]{1,2,0:T(8,128)(2,1)S(1)}, u32[]{:S(2)}, u32[]{:S(2)}) %collective-permute-start.3) | collective-permute-done | bytes 262176 | tf_op jit(solution)/shard_map/ppermute | solution.py:19
  109.8 7.5 %collective-permute-done.2 = bf16[4,256,128]{1,2,0:T(8,128)(2,1)S(1)} collective-permute-done((bf16[4,256,128]{1,2,0:T(8,128)(2,1)S(1)}, bf16[4,256,128]{1,2,0:T(8,128)(2,1)S(1)}, u32[]{:S(2)}, u32[]{:S(2)}) %collective-permute-start.2) | collective-permute-done | bytes 262176 | tf_op jit(solution)/shard_map/ppermute | solution.py:17
  117.3 1.0 pad_maximum_fusion.1
  118.4 27.4 %all-gather.14.cloned.1.call-done = bf16[12,1024,128]{1,2,0:T(8,128)(2,1)} async-done(((bf16[12,256,128]{1,2,0:T(8,128)(2,1)}), bf16[12,1024,128]{1,2,0:T(8,128)(2,1)}) %all-gather.14.cloned.1.call-update) | async-done | bytes 3145744 | tf_op jit(solution)/shard_map/all_gather | solution.py:44
  145.8 2.0 fusion.26
  147.8 1.8 convolution_add_fusion.13
  149.7 1.7 convolution_add_fusion.12
  151.4 0.5 convolution_add_fusion.11
  151.9 0.5 convolution_add_fusion.10
  152.4 0.5 convolution_add_fusion.9
  152.9 0.5 convolution_add_fusion.8
  153.4 1.2 fusion.7
  154.6 16.9 %all-gather.16.cloned.1.call-done = bf16[4,1024,128]{1,2,0:T(8,128)(2,1)} async-done(((bf16[4,256,128]{1,2,0:T(8,128)(2,1)}), bf16[4,1024,128]{1,2,0:T(8,128)(2,1)}) %all-gather.16.cloned.1.call-update) | async-done | bytes 1048592 | tf_op jit(solution)/shard_map/all_gather | solution.py:37
  171.6 2.1 fusion.10
  173.6 0.6 collective-permute-start.5
  174.2 1.5 collective-permute-start.4
  175.7 6.4 %collective-permute-done.5 = bf16[4,256,128]{1,2,0:T(8,128)(2,1)S(1)} collective-permute-done((bf16[4,256,128]{1,2,0:T(8,128)(2,1)S(1)}, bf16[4,256,128]{1,2,0:T(8,128)(2,1)S(1)}, u32[]{:S(2)}, u32[]{:S(2)}) %collective-permute-start.5) | collective-permute-done | bytes 262176 | tf_op jit(solution)/shard_map/ppermute | solution.py:19
  182.1 7.5 %collective-permute-done.4 = bf16[4,256,128]{1,2,0:T(8,128)(2,1)S(1)} collective-permute-done((bf16[4,256,128]{1,2,0:T(8,128)(2,1)S(1)}, bf16[4,256,128]{1,2,0:T(8,128)(2,1)S(1)}, u32[]{:S(2)}, u32[]{:S(2)}) %collective-permute-start.4) | collective-permute-done | bytes 262176 | tf_op jit(solution)/shard_map/ppermute | solution.py:17
  189.6 1.0 pad_maximum_fusion.2
  190.6 0.2 all-gather.20.cloned.1.call-start
  190.9 27.2 %all-gather.18.cloned.1.call-done = bf16[12,1024,128]{1,2,0:T(8,128)(2,1)} async-done(((bf16[12,256,128]{1,2,0:T(8,128)(2,1)}), bf16[12,1024,128]{1,2,0:T(8,128)(2,1)}) %all-gather.18.cloned.1.call-update) | async-done | bytes 3145744 | tf_op jit(solution)/shard_map/all_gather | solution.py:44
  218.1 2.0 fusion.17
  220.1 1.8 convolution_add_fusion.6
  222.0 1.7 convolution_add_fusion.5
  223.7 0.5 convolution_add_fusion.4
  224.2 0.5 convolution_add_fusion.3
  224.7 0.5 convolution_add_fusion.2
  225.2 0.5 convolution_add_fusion.1
  225.7 1.2 fusion.6
  226.9 16.9 %all-gather.20.cloned.1.call-done = bf16[4,1024,128]{1,2,0:T(8,128)(2,1)} async-done(((bf16[4,256,128]{1,2,0:T(8,128)(2,1)}), bf16[4,1024,128]{1,2,0:T(8,128)(2,1)}) %all-gather.20.cloned.1.call-update) | async-done | bytes 1048592 | tf_op jit(solution)/shard_map/all_gather | solution.py:37
  243.9 2.1 convolution_bitcast_fusion
  245.9 1.2 convolution_bitcast_fusion.1
  247.2 89.4 %all-reduce.2.cloned.1.call-done = f32[128,128]{0,1:T(8,128)} async-done(((f32[128,128]{0,1:T(8,128)}), f32[128,128]{0,1:T(8,128)}) %all-reduce.2.cloned.1.call-update) | async-done | bytes 65552 | tf_op jit(solution)/shard_map/psum | solution.py:67
  336.6 0.8 broadcast_multiply_fusion
  337.5 0.9 fusion.88
  338.4 11.7 %cholesky.16 = f32[128,128]{1,0:T(8,128)S(1)} custom-call(f32[128,128]{1,0:T(8,128)S(1)} %fusion.88), custom_call_target="Cholesky" | custom-call | tf_op jit(solution)/shard_map/jit(cholesky)/cholesky | solution.py:68
  350.2 0.6 compare_reduce_fusion
  350.8 0.7 fusion.89
  351.5 0.7 copy.13
  352.2 9.8 %custom-call.7 = f32[1,128,128]{1,2,0:T(8,128)S(1)} custom-call(f32[1,128,128]{2,1,0:T(8,128)S(1)} %get-tuple-element.5), custom_call_target="InvertDiagBlocksLowerTriangular" | custom-call | tf_op jit(solution)/shard_map/jit(_solve_triangular)/triangular_solve | solution.py:69
  362.0 1.8 fusion.86
  (41 shorter events, 0.8 us)
Async XLA Ops:
  7.2 20.3 %copy-start = (bf16[4,256,1024]{2,1,0:T(8,128)(2,1)S(1)}, bf16[4,256,1024]{2,1,0:T(8,128)(2,1)}, u32[]{:S(2)}) copy-start(bf16[4,256,1024]{2,1,0:T(8,128)(2,1)} %param.6) | copy-start | bytes 6291460
  7.2 20.3 %all-gather.8.cloned.1.call-start = ((), (), s32[]{:S(2)}) async-start(), calls=%async_computation | async-start | bytes 1310720 | tf_op jit(solution)/shard_map/all_gather | solution.py:37
  7.9 65.5 %all-gather.10.cloned.1.call-start = ((), (), s32[]{:S(2)}) async-start(), calls=%async_computation.1 | async-start | bytes 3932160 | tf_op jit(solution)/shard_map/all_gather | solution.py:44
  29.4 17.1 %copy-start.11 = (s32[4]{0:T(128)S(1)}, s32[4]{0:T(128)}, u32[]{:S(2)}) copy-start(s32[4]{0:T(128)} %param.9) | copy-start | bytes 52
  29.4 27.7 %copy-start.10 = (bf16[4,256,128]{2,1,0:T(8,128)(2,1)S(1)}, bf16[4,256,128]{2,1,0:T(8,128)(2,1)}, u32[]{:S(2)}) copy-start(bf16[4,256,128]{2,1,0:T(8,128)(2,1)} %param.5) | copy-start | bytes 786436
  29.4 8.5 %collective-permute-start.1 = (bf16[4,256,128]{2,1,0:T(8,128)(2,1)S(1)}, bf16[4,256,128]{2,1,0:T(8,128)(2,1)S(1)}, u32[]{:S(2)}, u32[]{:S(2)}) collective-permute-start(bf16[4,256,128]{2,1,0:T(8,128)(2,1)S(1)} %convolution_convert_fusion.2), channel_id=1, source_target_pairs={{4,0},{8,4},{12,8},{0,12},{5,1},{9,5},{13,9},{1,13},{6,2},{10,6},{... | collective-permute-start | bytes 786440 | tf_op jit(solution)/shard_map/ppermute | solution.py:19
  30.0 15.4 %collective-permute-start = (bf16[4,256,128]{2,1,0:T(8,128)(2,1)S(1)}, bf16[4,256,128]{2,1,0:T(8,128)(2,1)S(1)}, u32[]{:S(2)}, u32[]{:S(2)}) collective-permute-start(bf16[4,256,128]{2,1,0:T(8,128)(2,1)S(1)} %convolution_convert_fusion.2), channel_id=1, source_target_pairs={{0,4},{4,8},{8,12},{12,0},{1,5},{5,9},{9,13},{13,1},{2,6},{6,10},{... | collective-permute-start | bytes 786440 | tf_op jit(solution)/shard_map/ppermute | solution.py:17
  46.4 52.9 %all-gather.12.cloned.1.call-start = ((), (), s32[]{:S(2)}) async-start(), calls=%async_computation.2 | async-start | bytes 1310720 | tf_op jit(solution)/shard_map/all_gather | solution.py:37
  73.4 2.1 copy-start.1
  75.5 3.6 copy-start.4
  75.5 3.6 copy-start.7
  82.3 63.5 %all-gather.14.cloned.1.call-start = ((), (), s32[]{:S(2)}) async-start(), calls=%async_computation.3 | async-start | bytes 3932160 | tf_op jit(solution)/shard_map/all_gather | solution.py:44
  101.3 8.5 %collective-permute-start.3 = (bf16[4,256,128]{1,2,0:T(8,128)(2,1)S(1)}, bf16[4,256,128]{1,2,0:T(8,128)(2,1)S(1)}, u32[]{:S(2)}, u32[]{:S(2)}) collective-permute-start(bf16[4,256,128]{1,2,0:T(8,128)(2,1)S(1)} %fusion.9), channel_id=1, source_target_pairs={{4,0},{8,4},{12,8},{0,12},{5,1},{9,5},{13,9},{1,13},{6,2},{10,6},{... | collective-permute-start | bytes 786440 | tf_op jit(solution)/shard_map/ppermute | solution.py:19
  101.9 15.4 %collective-permute-start.2 = (bf16[4,256,128]{1,2,0:T(8,128)(2,1)S(1)}, bf16[4,256,128]{1,2,0:T(8,128)(2,1)S(1)}, u32[]{:S(2)}, u32[]{:S(2)}) collective-permute-start(bf16[4,256,128]{1,2,0:T(8,128)(2,1)S(1)} %fusion.9), channel_id=1, source_target_pairs={{0,4},{4,8},{8,12},{12,0},{1,5},{5,9},{9,13},{13,1},{2,6},{6,10},{... | collective-permute-start | bytes 786440 | tf_op jit(solution)/shard_map/ppermute | solution.py:17
  118.3 53.2 %all-gather.16.cloned.1.call-start = ((), (), s32[]{:S(2)}) async-start(), calls=%async_computation.4 | async-start | bytes 1310720 | tf_op jit(solution)/shard_map/all_gather | solution.py:37
  145.8 2.1 copy-start.2
  147.8 3.6 copy-start.6
  147.8 3.6 copy-start.8
  154.6 63.5 %all-gather.18.cloned.1.call-start = ((), (), s32[]{:S(2)}) async-start(), calls=%async_computation.5 | async-start | bytes 3932160 | tf_op jit(solution)/shard_map/all_gather | solution.py:44
  173.6 8.5 %collective-permute-start.5 = (bf16[4,256,128]{1,2,0:T(8,128)(2,1)S(1)}, bf16[4,256,128]{1,2,0:T(8,128)(2,1)S(1)}, u32[]{:S(2)}, u32[]{:S(2)}) collective-permute-start(bf16[4,256,128]{1,2,0:T(8,128)(2,1)S(1)} %fusion.10), channel_id=1, source_target_pairs={{4,0},{8,4},{12,8},{0,12},{5,1},{9,5},{13,9},{1,13},{6,2},{10,6},{... | collective-permute-start | bytes 786440 | tf_op jit(solution)/shard_map/ppermute | solution.py:19
  174.2 15.4 %collective-permute-start.4 = (bf16[4,256,128]{1,2,0:T(8,128)(2,1)S(1)}, bf16[4,256,128]{1,2,0:T(8,128)(2,1)S(1)}, u32[]{:S(2)}, u32[]{:S(2)}) collective-permute-start(bf16[4,256,128]{1,2,0:T(8,128)(2,1)S(1)} %fusion.10), channel_id=1, source_target_pairs={{0,4},{4,8},{8,12},{12,0},{1,5},{5,9},{9,13},{13,1},{2,6},{6,10},{... | collective-permute-start | bytes 786440 | tf_op jit(solution)/shard_map/ppermute | solution.py:17
  190.6 53.2 %all-gather.20.cloned.1.call-start = ((), (), s32[]{:S(2)}) async-start(), calls=%async_computation.6 | async-start | bytes 1310720 | tf_op jit(solution)/shard_map/all_gather | solution.py:37
  218.1 2.1 copy-start.3
  220.1 3.6 copy-start.5
  220.1 3.6 copy-start.9
  226.9 109.7 %all-reduce.2.cloned.1.call-start = ((), (), s32[]{:S(2)}) async-start(), calls=%async_computation.7 | async-start | bytes 131072 | tf_op jit(solution)/shard_map/psum | solution.py:67
Sparse Core Ops, SparseCore 0:
  9.5 17.8 all-gather.7
  46.5 26.8 all-gather.9
  82.4 16.8 all-gather.11
  118.5 27.2 all-gather.13
  154.7 16.8 all-gather.15
  190.8 27.2 all-gather.17
  227.0 16.8 all-gather.19
  247.9 88.6 all-reduce.1
where the time goes:
time: 371 us
  waiting for transfers between devices  273 us (74%)
  matrix products  37.1 us (10%)
  other arithmetic  27.5 us (7%)
  between operations  24.5 us (7%)
  starting transfers between devices  6.74 us (2%)
    psum x1, waiting for transfers between devices, body(): gram = lax.psum(local_gram, ('harm', 'wall')) / count  89.4 us
    all_gather x3, waiting for transfers between devices, body(): add_piece = lax.all_gather(extended, 'wall', axis=1, tiled=True)  70.7 us
    all_gather x4, waiting for transfers between devices, apply_inverse(): return add_inverse(lax.all_gather(source, 'wall', axis=1, tiled=True))  70.3 us
    ppermute x3, waiting for transfers between devices, padded(): lax.ppermute(tail, axis, [(i, (i + 1) % count) for i in range(count)])  22.5 us
    ppermute x3, waiting for transfers between devices, padded(): lax.ppermute(head, axis, [((i + 1) % count, i) for i in range(count)])  19.3 us
    dot_general x12, matrix products, body(): jnp.einsum('rc,hck->hrk', up_cols, below, preferred_element_type=jnp.floa...  13.6 us
    dot_general x12, matrix products, body(): jnp.einsum('rc,hck->hrk', down_cols, above, preferred_element_type=jnp.fl...  12.4 us
    another operation x3, other arithmetic, body(): lower = jnp.linalg.cholesky(gram)  12.4 us
  transfers between devices with their start and end apart: 14, of which 14 were waited for; matrix products, arithmetic and copies ran while one was open for 0% of the time, Pallas kernels for 0%

commit v1 on v0

--- a/solution.py
+++ b/solution.py
@@ -64,7 +64,7 @@
     local_gram = jnp.dot(
         flat.T, flat, precision=lax.Precision.HIGHEST, preferred_element_type=jnp.float32
     )
-    gram = lax.psum(local_gram, ("harm", "wall")) / count
+    gram = jnp.sum(lax.all_gather(local_gram, ("harm", "wall")), axis=0) / count
     lower = jnp.linalg.cholesky(gram)
     basis = jax.scipy.linalg.solve_triangular(lower, flat.T, lower=True).T
     triangle = lower.T

time: 371 us -> 321 us (0.87)
  waiting for transfers between devices: 273 us -> 220 us
    psum x1 -> x0, waiting for transfers between devices: 89.4 us -> none  [body(): gram = lax.psum(local_gram, ('harm', 'wall')) / count]
    all_gather x0 -> x1, waiting for transfers between devices: none -> 37 us  [body(): gram = jnp.sum(lax.all_gather(local_gram, ('harm', 'wall')), axis=0) / count]
where the time goes in v1:
time: 321 us; the launch traced here: 318 us
  waiting for transfers between devices  220 us (69%)
  matrix products  37.1 us (12%)
  other arithmetic  27.1 us (8%)
  between operations  24.5 us (8%)
  starting transfers between devices  6.74 us (2%)
    all_gather x3, waiting for transfers between devices, body(): add_piece = lax.all_gather(extended, 'wall', axis=1, tiled=True)  70.7 us
    all_gather x4, waiting for transfers between devices, apply_inverse(): return add_inverse(lax.all_gather(source, 'wall', axis=1, tiled=True))  70.3 us
    all_gather x1, waiting for transfers between devices, body(): gram = jnp.sum(lax.all_gather(local_gram, ('harm', 'wall')), axis=0) / count  37 us
    ppermute x3, waiting for transfers between devices, padded(): lax.ppermute(tail, axis, [(i, (i + 1) % count) for i in range(count)])  22.5 us
    ppermute x3, waiting for transfers between devices, padded(): lax.ppermute(head, axis, [((i + 1) % count, i) for i in range(count)])  19.3 us
    dot_general x12, matrix products, body(): jnp.einsum('rc,hck->hrk', up_cols, below, preferred_element_type=jnp.floa...  13.6 us
    dot_general x12, matrix products, body(): jnp.einsum('rc,hck->hrk', down_cols, above, preferred_element_type=jnp.fl...  12.4 us
    another operation x3, other arithmetic, body(): lower = jnp.linalg.cholesky(gram)  12.4 us
  transfers between devices with their start and end apart: 14, of which 14 were waited for; matrix products, arithmetic and copies ran while one was open for 0% of the time, Pallas kernels for 0%

profile of v1, /device:TPU:8, one launch (start us, length us, event | category | flops | bytes accessed | tf_op | source)
XLA Modules:
  0.0 317.8 jit_solution(14829234867465790897)
XLA Ops:
  7.2 0.7 all-gather.10.cloned.1.call-update
  8.0 19.5 %all-gather.10.cloned.1.call-done = bf16[4,1024,128]{2,1,0:T(8,128)(2,1)} async-done(((bf16[4,256,128]{2,1,0:T(8,128)(2,1)}), bf16[4,1024,128]{2,1,0:T(8,128)(2,1)}) %all-gather.10.cloned.1.call-update) | async-done | bytes 1048592 | tf_op jit(solution)/shard_map/all_gather | solution.py:37
  27.4 1.9 convolution_convert_fusion.2
  29.4 0.6 collective-permute-start.1
  30.0 1.5 collective-permute-start
  31.5 6.4 %collective-permute-done.1 = bf16[4,256,128]{2,1,0:T(8,128)(2,1)S(1)} collective-permute-done((bf16[4,256,128]{2,1,0:T(8,128)(2,1)S(1)}, bf16[4,256,128]{2,1,0:T(8,128)(2,1)S(1)}, u32[]{:S(2)}, u32[]{:S(2)}) %collective-permute-start.1) | collective-permute-done | bytes 262176 | tf_op jit(solution)/shard_map/ppermute | solution.py:19
  37.9 7.5 %collective-permute-done = bf16[4,256,128]{2,1,0:T(8,128)(2,1)S(1)} collective-permute-done((bf16[4,256,128]{2,1,0:T(8,128)(2,1)S(1)}, bf16[4,256,128]{2,1,0:T(8,128)(2,1)S(1)}, u32[]{:S(2)}, u32[]{:S(2)}) %collective-permute-start) | collective-permute-done | bytes 262176 | tf_op jit(solution)/shard_map/ppermute | solution.py:17
  45.4 1.0 pad_maximum_fusion
  46.4 0.7 fusion.114
  57.1 0.1 copy.13
  57.3 16.1 %all-gather.12.cloned.1.call-done = bf16[12,1024,128]{2,1,0:T(8,128)(2,1)} async-done(((bf16[12,256,128]{2,1,0:T(8,128)(2,1)}), bf16[12,1024,128]{2,1,0:T(8,128)(2,1)}) %all-gather.12.cloned.1.call-update) | async-done | bytes 3145744 | tf_op jit(solution)/shard_map/all_gather | solution.py:44
  73.4 2.0 fusion.35
  75.5 1.9 convolution_add_fusion.20
  77.3 1.7 convolution_add_fusion.19
  79.1 0.5 convolution_add_fusion.18
  79.6 0.5 convolution_add_fusion.17
  80.1 0.5 convolution_add_fusion.16
  80.6 0.5 convolution_add_fusion.15
  81.1 1.2 fusion.8
  82.3 16.9 %all-gather.14.cloned.1.call-done = bf16[4,1024,128]{1,2,0:T(8,128)(2,1)} async-done(((bf16[4,256,128]{1,2,0:T(8,128)(2,1)}), bf16[4,1024,128]{1,2,0:T(8,128)(2,1)}) %all-gather.14.cloned.1.call-update) | async-done | bytes 1048592 | tf_op jit(solution)/shard_map/all_gather | solution.py:37
  99.3 2.1 fusion.9
  101.3 0.6 collective-permute-start.3
  101.9 1.5 collective-permute-start.2
  103.4 6.4 %collective-permute-done.3 = bf16[4,256,128]{1,2,0:T(8,128)(2,1)S(1)} collective-permute-done((bf16[4,256,128]{1,2,0:T(8,128)(2,1)S(1)}, bf16[4,256,128]{1,2,0:T(8,128)(2,1)S(1)}, u32[]{:S(2)}, u32[]{:S(2)}) %collective-permute-start.3) | collective-permute-done | bytes 262176 | tf_op jit(solution)/shard_map/ppermute | solution.py:19
  109.8 7.5 %collective-permute-done.2 = bf16[4,256,128]{1,2,0:T(8,128)(2,1)S(1)} collective-permute-done((bf16[4,256,128]{1,2,0:T(8,128)(2,1)S(1)}, bf16[4,256,128]{1,2,0:T(8,128)(2,1)S(1)}, u32[]{:S(2)}, u32[]{:S(2)}) %collective-permute-start.2) | collective-permute-done | bytes 262176 | tf_op jit(solution)/shard_map/ppermute | solution.py:17
  117.3 1.0 pad_maximum_fusion.1
  118.4 27.4 %all-gather.16.cloned.1.call-done = bf16[12,1024,128]{1,2,0:T(8,128)(2,1)} async-done(((bf16[12,256,128]{1,2,0:T(8,128)(2,1)}), bf16[12,1024,128]{1,2,0:T(8,128)(2,1)}) %all-gather.16.cloned.1.call-update) | async-done | bytes 3145744 | tf_op jit(solution)/shard_map/all_gather | solution.py:44
  145.8 2.0 fusion.26
  147.8 1.8 convolution_add_fusion.13
  149.7 1.7 convolution_add_fusion.12
  151.4 0.5 convolution_add_fusion.11
  151.9 0.5 convolution_add_fusion.10
  152.4 0.5 convolution_add_fusion.9
  152.9 0.5 convolution_add_fusion.8
  153.4 1.2 fusion.7
  154.6 16.9 %all-gather.18.cloned.1.call-done = bf16[4,1024,128]{1,2,0:T(8,128)(2,1)} async-done(((bf16[4,256,128]{1,2,0:T(8,128)(2,1)}), bf16[4,1024,128]{1,2,0:T(8,128)(2,1)}) %all-gather.18.cloned.1.call-update) | async-done | bytes 1048592 | tf_op jit(solution)/shard_map/all_gather | solution.py:37
  171.6 2.1 fusion.10
  173.6 0.6 collective-permute-start.5
  174.2 1.5 collective-permute-start.4
  175.7 6.4 %collective-permute-done.5 = bf16[4,256,128]{1,2,0:T(8,128)(2,1)S(1)} collective-permute-done((bf16[4,256,128]{1,2,0:T(8,128)(2,1)S(1)}, bf16[4,256,128]{1,2,0:T(8,128)(2,1)S(1)}, u32[]{:S(2)}, u32[]{:S(2)}) %collective-permute-start.5) | collective-permute-done | bytes 262176 | tf_op jit(solution)/shard_map/ppermute | solution.py:19
  182.1 7.5 %collective-permute-done.4 = bf16[4,256,128]{1,2,0:T(8,128)(2,1)S(1)} collective-permute-done((bf16[4,256,128]{1,2,0:T(8,128)(2,1)S(1)}, bf16[4,256,128]{1,2,0:T(8,128)(2,1)S(1)}, u32[]{:S(2)}, u32[]{:S(2)}) %collective-permute-start.4) | collective-permute-done | bytes 262176 | tf_op jit(solution)/shard_map/ppermute | solution.py:17
  189.6 1.0 pad_maximum_fusion.2
  190.6 0.2 all-gather.22.cloned.1.call-start
  190.9 27.2 %all-gather.20.cloned.1.call-done = bf16[12,1024,128]{1,2,0:T(8,128)(2,1)} async-done(((bf16[12,256,128]{1,2,0:T(8,128)(2,1)}), bf16[12,1024,128]{1,2,0:T(8,128)(2,1)}) %all-gather.20.cloned.1.call-update) | async-done | bytes 3145744 | tf_op jit(solution)/shard_map/all_gather | solution.py:44
  218.1 2.0 fusion.17
  220.1 1.8 convolution_add_fusion.6
  222.0 1.7 convolution_add_fusion.5
  223.7 0.5 convolution_add_fusion.4
  224.2 0.5 convolution_add_fusion.3
  224.7 0.5 convolution_add_fusion.2
  225.2 0.5 convolution_add_fusion.1
  225.7 1.2 fusion.6
  226.9 16.9 %all-gather.22.cloned.1.call-done = bf16[4,1024,128]{1,2,0:T(8,128)(2,1)} async-done(((bf16[4,256,128]{1,2,0:T(8,128)(2,1)}), bf16[4,1024,128]{1,2,0:T(8,128)(2,1)}) %all-gather.22.cloned.1.call-update) | async-done | bytes 1048592 | tf_op jit(solution)/shard_map/all_gather | solution.py:37
  243.9 2.1 convolution_bitcast_fusion
  245.9 1.2 convolution_bitcast_fusion.1
  247.2 37.0 %all-gather.24.cloned.1.call-done = f32[2048,128]{1,0:T(8,128)} async-done(((f32[128,128]{1,0:T(8,128)}), f32[2048,128]{1,0:T(8,128)}) %all-gather.24.cloned.1.call-update) | async-done | bytes 1048592 | tf_op jit(solution)/shard_map/all_gather | solution.py:67
  284.1 1.3 reduce_sum.11
  285.4 0.1 copy.15
  285.5 11.7 %cholesky.16 = f32[128,128]{1,0:T(8,128)S(1)} custom-call(f32[128,128]{1,0:T(8,128)S(1)} %fusion.88), custom_call_target="Cholesky" | custom-call | tf_op jit(solution)/shard_map/jit(cholesky)/cholesky | solution.py:68
  297.3 0.6 compare_reduce_fusion
  297.9 0.7 fusion.89
  298.6 0.7 copy.18
  299.3 9.8 %custom-call.7 = f32[1,128,128]{1,2,0:T(8,128)S(1)} custom-call(f32[1,128,128]{2,1,0:T(8,128)S(1)} %get-tuple-element.7), custom_call_target="InvertDiagBlocksLowerTriangular" | custom-call | tf_op jit(solution)/shard_map/jit(_solve_triangular)/triangular_solve | solution.py:69
  309.1 1.8 fusion.86
  (41 shorter events, 0.7 us)
Async XLA Ops:
  7.2 20.3 %copy-start = (bf16[4,256,1024]{2,1,0:T(8,128)(2,1)S(1)}, bf16[4,256,1024]{2,1,0:T(8,128)(2,1)}, u32[]{:S(2)}) copy-start(bf16[4,256,1024]{2,1,0:T(8,128)(2,1)} %param.6) | copy-start | bytes 6291460
  7.2 20.3 %all-gather.10.cloned.1.call-start = ((), (), s32[]{:S(2)}) async-start(), calls=%async_computation | async-start | bytes 1310720 | tf_op jit(solution)/shard_map/all_gather | solution.py:37
  7.9 65.5 %all-gather.12.cloned.1.call-start = ((), (), s32[]{:S(2)}) async-start(), calls=%async_computation.1 | async-start | bytes 3932160 | tf_op jit(solution)/shard_map/all_gather | solution.py:44
  29.4 17.1 %copy-start.11 = (s32[4]{0:T(128)S(1)}, s32[4]{0:T(128)}, u32[]{:S(2)}) copy-start(s32[4]{0:T(128)} %param.9) | copy-start | bytes 52
  29.4 27.7 %copy-start.10 = (bf16[4,256,128]{2,1,0:T(8,128)(2,1)S(1)}, bf16[4,256,128]{2,1,0:T(8,128)(2,1)}, u32[]{:S(2)}) copy-start(bf16[4,256,128]{2,1,0:T(8,128)(2,1)} %param.5) | copy-start | bytes 786436
  29.4 8.5 %collective-permute-start.1 = (bf16[4,256,128]{2,1,0:T(8,128)(2,1)S(1)}, bf16[4,256,128]{2,1,0:T(8,128)(2,1)S(1)}, u32[]{:S(2)}, u32[]{:S(2)}) collective-permute-start(bf16[4,256,128]{2,1,0:T(8,128)(2,1)S(1)} %convolution_convert_fusion.2), channel_id=1, source_target_pairs={{4,0},{8,4},{12,8},{0,12},{5,1},{9,5},{13,9},{1,13},{6,2},{10,6},{... | collective-permute-start | bytes 786440 | tf_op jit(solution)/shard_map/ppermute | solution.py:19
  30.0 15.4 %collective-permute-start = (bf16[4,256,128]{2,1,0:T(8,128)(2,1)S(1)}, bf16[4,256,128]{2,1,0:T(8,128)(2,1)S(1)}, u32[]{:S(2)}, u32[]{:S(2)}) collective-permute-start(bf16[4,256,128]{2,1,0:T(8,128)(2,1)S(1)} %convolution_convert_fusion.2), channel_id=1, source_target_pairs={{0,4},{4,8},{8,12},{12,0},{1,5},{5,9},{9,13},{13,1},{2,6},{6,10},{... | collective-permute-start | bytes 786440 | tf_op jit(solution)/shard_map/ppermute | solution.py:17
  46.4 52.9 %all-gather.14.cloned.1.call-start = ((), (), s32[]{:S(2)}) async-start(), calls=%async_computation.2 | async-start | bytes 1310720 | tf_op jit(solution)/shard_map/all_gather | solution.py:37
  73.4 2.1 copy-start.1
  75.5 3.6 %copy-start.4 = (bf16[12,1024,128]{2,1,0:T(8,128)(2,1)S(1)}, bf16[12,1024,128]{2,1,0:T(8,128)(2,1)}, u32[]{:S(2)}) copy-start(bf16[12,1024,128]{2,1,0:T(8,128)(2,1)} %all-gather.12.cloned.1.call-done) | copy-start | bytes 9437188
  75.5 3.6 %copy-start.7 = (bf16[4,256,1024]{2,1,0:T(8,128)(2,1)S(1)}, bf16[4,256,1024]{2,1,0:T(8,128)(2,1)}, u32[]{:S(2)}) copy-start(bf16[4,256,1024]{2,1,0:T(8,128)(2,1)} %param.8) | copy-start | bytes 6291460
  82.3 63.5 %all-gather.16.cloned.1.call-start = ((), (), s32[]{:S(2)}) async-start(), calls=%async_computation.3 | async-start | bytes 3932160 | tf_op jit(solution)/shard_map/all_gather | solution.py:44
  101.3 8.5 %collective-permute-start.3 = (bf16[4,256,128]{1,2,0:T(8,128)(2,1)S(1)}, bf16[4,256,128]{1,2,0:T(8,128)(2,1)S(1)}, u32[]{:S(2)}, u32[]{:S(2)}) collective-permute-start(bf16[4,256,128]{1,2,0:T(8,128)(2,1)S(1)} %fusion.9), channel_id=1, source_target_pairs={{4,0},{8,4},{12,8},{0,12},{5,1},{9,5},{13,9},{1,13},{6,2},{10,6},{... | collective-permute-start | bytes 786440 | tf_op jit(solution)/shard_map/ppermute | solution.py:19
  101.9 15.4 %collective-permute-start.2 = (bf16[4,256,128]{1,2,0:T(8,128)(2,1)S(1)}, bf16[4,256,128]{1,2,0:T(8,128)(2,1)S(1)}, u32[]{:S(2)}, u32[]{:S(2)}) collective-permute-start(bf16[4,256,128]{1,2,0:T(8,128)(2,1)S(1)} %fusion.9), channel_id=1, source_target_pairs={{0,4},{4,8},{8,12},{12,0},{1,5},{5,9},{9,13},{13,1},{2,6},{6,10},{... | collective-permute-start | bytes 786440 | tf_op jit(solution)/shard_map/ppermute | solution.py:17
  118.3 53.2 %all-gather.18.cloned.1.call-start = ((), (), s32[]{:S(2)}) async-start(), calls=%async_computation.4 | async-start | bytes 1310720 | tf_op jit(solution)/shard_map/all_gather | solution.py:37
  145.8 2.1 copy-start.2
  147.8 3.6 %copy-start.6 = (bf16[12,1024,128]{1,2,0:T(8,128)(2,1)S(1)}, bf16[12,1024,128]{1,2,0:T(8,128)(2,1)}, u32[]{:S(2)}) copy-start(bf16[12,1024,128]{1,2,0:T(8,128)(2,1)} %all-gather.16.cloned.1.call-done) | copy-start | bytes 9437188
  147.8 3.6 %copy-start.8 = (bf16[4,256,1024]{2,1,0:T(8,128)(2,1)S(1)}, bf16[4,256,1024]{2,1,0:T(8,128)(2,1)}, u32[]{:S(2)}) copy-start(bf16[4,256,1024]{2,1,0:T(8,128)(2,1)} %param.8) | copy-start | bytes 6291460
  154.6 63.5 %all-gather.20.cloned.1.call-start = ((), (), s32[]{:S(2)}) async-start(), calls=%async_computation.5 | async-start | bytes 3932160 | tf_op jit(solution)/shard_map/all_gather | solution.py:44
  173.6 8.5 %collective-permute-start.5 = (bf16[4,256,128]{1,2,0:T(8,128)(2,1)S(1)}, bf16[4,256,128]{1,2,0:T(8,128)(2,1)S(1)}, u32[]{:S(2)}, u32[]{:S(2)}) collective-permute-start(bf16[4,256,128]{1,2,0:T(8,128)(2,1)S(1)} %fusion.10), channel_id=1, source_target_pairs={{4,0},{8,4},{12,8},{0,12},{5,1},{9,5},{13,9},{1,13},{6,2},{10,6},{... | collective-permute-start | bytes 786440 | tf_op jit(solution)/shard_map/ppermute | solution.py:19
  174.2 15.4 %collective-permute-start.4 = (bf16[4,256,128]{1,2,0:T(8,128)(2,1)S(1)}, bf16[4,256,128]{1,2,0:T(8,128)(2,1)S(1)}, u32[]{:S(2)}, u32[]{:S(2)}) collective-permute-start(bf16[4,256,128]{1,2,0:T(8,128)(2,1)S(1)} %fusion.10), channel_id=1, source_target_pairs={{0,4},{4,8},{8,12},{12,0},{1,5},{5,9},{9,13},{13,1},{2,6},{6,10},{... | collective-permute-start | bytes 786440 | tf_op jit(solution)/shard_map/ppermute | solution.py:17
  190.6 53.2 %all-gather.22.cloned.1.call-start = ((), (), s32[]{:S(2)}) async-start(), calls=%async_computation.6 | async-start | bytes 1310720 | tf_op jit(solution)/shard_map/all_gather | solution.py:37
  218.1 2.1 copy-start.3
  220.1 3.6 %copy-start.5 = (bf16[12,1024,128]{1,2,0:T(8,128)(2,1)S(1)}, bf16[12,1024,128]{1,2,0:T(8,128)(2,1)}, u32[]{:S(2)}) copy-start(bf16[12,1024,128]{1,2,0:T(8,128)(2,1)} %all-gather.20.cloned.1.call-done) | copy-start | bytes 9437188
  220.1 3.6 %copy-start.9 = (bf16[4,256,1024]{2,1,0:T(8,128)(2,1)S(1)}, bf16[4,256,1024]{2,1,0:T(8,128)(2,1)}, u32[]{:S(2)}) copy-start(bf16[4,256,1024]{2,1,0:T(8,128)(2,1)} %param.8) | copy-start | bytes 6291460
  226.9 57.3 %all-gather.24.cloned.1.call-start = ((), (), s32[]{:S(2)}) async-start(), calls=%async_computation.7 | async-start | bytes 1114112 | tf_op jit(solution)/shard_map/all_gather | solution.py:67
Sparse Core Ops, SparseCore 0:
  9.5 17.8 all-gather.9
  46.5 26.8 all-gather.11
  82.4 16.8 all-gather.13
  118.5 27.2 all-gather.15
  154.7 16.8 all-gather.17
  190.8 27.2 all-gather.19
  227.0 16.8 all-gather.21
  247.3 36.8 all-gather.23
